TPU v7x, 256 devices: a whole 4x4x8 slice. The times are simulated.
256 devices in a mesh: group: 8 (over y, core), tile: 32 (over z, x).
Axes of the slice: x: 4, y: 4, z: 8, core: 2. Of those that a mesh axis runs over, the one named last changes fastest.
Arguments:
- radiance: bfloat16 [224, 3072, 1024], P(None, 'tile', 'group'), may hold values from -200 to 200
- valid_mask: int32 [3072, 1024], P('tile', 'group'), may hold values 0 or 1
Outputs:
- whitened: bfloat16 [224, 3072, 1024], P(None, 'tile', 'group')
- whitened_cov: float32 [224, 224], replicated
All inputs are finite; a program needn't handle non-finite values. No bound on the sum of `valid_mask` on one device may be relied on, other than what follows from the above.
Results may differ from a plain program's by a relative error of at most 0.0058.
Values may be sent and summed in bfloat16 or wider, within the bound.
No kernel may reach another device: no remote copies, remote signals or barrier semaphores. Data moves between devices by JAX's collectives and lax.ppermute only.
A program may use at most 128 MiB of HBM per device.

v0:
```python
import jax
import jax.numpy as jnp
from jax import lax
from jax.sharding import PartitionSpec as P


def padded_2(block, sides, width):
    for axis, dim in sides:
        count = lax.axis_size(axis)
        forward = [(i, i + 1) for i in range(count - 1)]
        backward = [(target, source) for source, target in forward]
        low = lax.ppermute(
            lax.slice_in_dim(block, block.shape[dim] - width, None, axis=dim), axis, forward
        )
        high = lax.ppermute(lax.slice_in_dim(block, 0, width, axis=dim), axis, backward)
        block = jnp.concatenate([low, block, high], axis=dim)
    return block


def smooth_noise(padded, rows, cols):
    field = padded.astype(jnp.float32)
    row_smooth = (
        field[:, 0:rows]
        + 4.0 * field[:, 1 : rows + 1]
        + 6.0 * field[:, 2 : rows + 2]
        + 4.0 * field[:, 3 : rows + 3]
        + field[:, 4 : rows + 4]
    ) / 16.0
    smooth = (
        row_smooth[:, :, 0:cols]
        + 4.0 * row_smooth[:, :, 1 : cols + 1]
        + 6.0 * row_smooth[:, :, 2 : cols + 2]
        + 4.0 * row_smooth[:, :, 3 : cols + 3]
        + row_smooth[:, :, 4 : cols + 4]
    ) / 16.0
    centre = field[:, 2 : rows + 2, 2 : cols + 2]
    noise = centre - 0.5 * (
        field[:, 1 : rows + 1, 2 : cols + 2] + field[:, 3 : rows + 3, 2 : cols + 2]
    )
    return (smooth, noise)


def finish(signal_moment, noise_moment, signal_first, noise_first, count):
    signal_cov = (signal_moment - jnp.outer(signal_first, signal_first) / count) / (count - 1.0)
    noise_cov = (noise_moment - jnp.outer(noise_first, noise_first) / count) / (count - 1.0)
    lower = jnp.linalg.cholesky(noise_cov)
    identity = jnp.eye(signal_first.shape[0], dtype=jnp.float32)
    inverse_lower = jax.scipy.linalg.solve_triangular(lower, identity, lower=True)
    left = jnp.dot(inverse_lower, signal_cov, precision=lax.Precision.HIGHEST)
    whitened_cov = jnp.dot(left, inverse_lower.T, precision=lax.Precision.HIGHEST)
    return (inverse_lower, whitened_cov)


def body(radiance, valid_mask):
    bands, rows, cols = radiance.shape
    padded = padded_2(radiance, (("group", 2), ("tile", 1)), 2)
    smooth, noise = smooth_noise(padded, rows, cols)
    weight = valid_mask.astype(jnp.float32)[None]
    signal_masked = smooth * weight
    noise_masked = noise * weight
    signal_first = jnp.sum(signal_masked, axis=(1, 2))
    noise_first = jnp.sum(noise_masked, axis=(1, 2))
    count = jnp.sum(weight)
    signal_flat = signal_masked.astype(jnp.bfloat16).reshape(bands, rows * cols)
    noise_flat = noise_masked.astype(jnp.bfloat16).reshape(bands, rows * cols)
    dims = (((1,), (1,)), ((), ()))
    signal_moment = lax.dot_general(
        signal_flat, signal_flat, dims, preferred_element_type=jnp.float32
    )
    noise_moment = lax.dot_general(noise_flat, noise_flat, dims, preferred_element_type=jnp.float32)
    count_column = jnp.full((bands,), count, jnp.float32)
    block = jnp.concatenate([signal_moment, noise_moment], axis=1)
    side = jnp.stack([signal_first, noise_first, count_column], axis=1)
    total_block, total_side = lax.psum((block, side), ("group", "tile"))
    signal_total = total_block[:, :bands]
    noise_total = total_block[:, bands:]
    count_total = total_side[0, 2]
    signal_sum = total_side[:, 0]
    inverse_lower, whitened_cov = finish(
        signal_total, noise_total, signal_sum, total_side[:, 1], count_total
    )
    inverse_cast = inverse_lower.astype(jnp.bfloat16)
    mean_signal = signal_sum / count_total
    centered = (
        (weight * (smooth - mean_signal[:, None, None]))
        .astype(jnp.bfloat16)
        .reshape(bands, rows * cols)
    )
    product = jnp.dot(inverse_cast, centered, preferred_element_type=jnp.float32)
    whitened = product.astype(jnp.bfloat16).reshape(bands, rows, cols)
    return (whitened, whitened_cov)


def solution(mesh):
    return jax.shard_map(
        body,
        mesh=mesh,
        in_specs=(P(None, "tile", "group"), P("tile", "group")),
        out_specs=(P(None, "tile", "group"), P()),
        check_vma=False,
    )
```

profile of v0, /device:TPU:6, one launch (start us, length us, event | category | flops | bytes accessed | tf_op | source)
XLA Modules:
  0.0 533.3 jit_solution(12199069908704797337)
XLA Ops:
  7.2 10.8 %fusion.46 = (bf16[224,96,2]{2,1,0:T(8,128)(2,1)}, bf16[224,96,2]{2,1,0:T(8,128)(2,1)}) fusion(bf16[224,96,128]{2,1,0:T(8,128)(2,1)} %param.2), kind=kLoop, calls=%fused_computation.90 | loop fusion | bytes 344064 | tf_op jit(solution)/shard_map/slice | solution.py:13
  18.0 5.8 %copy.33 = bf16[224,96,2]{0,1,2:T(8,128)(2,1)S(1)} copy(bf16[224,96,2]{2,1,0:T(8,128)(2,1)} %get-tuple-element.29) | data formatting | bytes 172032
  25.2 5.8 %copy.32 = bf16[224,96,2]{0,1,2:T(8,128)(2,1)S(1)} copy(bf16[224,96,2]{2,1,0:T(8,128)(2,1)} %get-tuple-element.28) | data formatting | bytes 172032
  31.0 3.0 collective-permute-start
  34.0 9.3 %copy.19 = bf16[224,96,128]{0,2,1:T(8,128)(2,1)} copy(bf16[224,96,128]{2,1,0:T(8,128)(2,1)} %param.2) | data formatting | bytes 11010048 | tf_op args[0]
  45.3 3.7 collective-permute-start.2
  49.0 2.3 collective-permute-start.3
  53.5 6.0 %collective-permute-done.3 = bf16[224,2,132]{0,2,1:T(8,128)(2,1)S(1)} collective-permute-done((bf16[224,2,132]{0,2,1:T(8,128)(2,1)S(1)}, bf16[224,2,132]{0,2,1:T(8,128)(2,1)S(1)}, u32[]{:S(2)}, u32[]{:S(2)}) %collective-permute-start.3) | collective-permute-done | bytes 118304 | tf_op jit(solution)/shard_map/ppermute | solution.py:15
  59.5 8.8 %maximum_convert_fusion = f32[224,100,132]{0,2,1:T(8,128)S(1)} fusion(bf16[224,2,132]{0,2,1:T(8,128)(2,1)S(1)} %collective-permute-done.3, bf16[224,96,2]{0,2,1:T(2,128)(2,1)S(1)} %copy.20, bf16[224,96,128]{0,2,1:T(8,128)(2,1)} %copy.19, bf16[224,96,2]{0,2,1:T(2,128)(2,1)S(1)} %copy.18, bf16[224,2,132]{0,2,1:T(8,128)(2,1)S(1)} %collective-permute-done.2), kind=kLoop, calls=%fused_computation.23 | loop fusion | flops 29568000 | bytes 17740800 | tf_op jit(solution)/shard_map/convert_element_type | solution.py:21
  68.3 8.0 %fusion = f32[224,96,132]{0,2,1:T(8,128)} fusion(f32[224,100,132]{0,2,1:T(8,128)S(1)} %maximum_convert_fusion), kind=kLoop, calls=%fused_computation.2 | loop fusion | flops 22708224 | bytes 68124672 | tf_op jit(solution)/shard_map/div | solution.py:22
  76.3 7.3 %fusion.44 = (f32[224]{0:T(256)S(1)}, bf16[224,96,128]{0,2,1:T(8,128)(2,1)}) fusion(f32[96,128]{1,0:T(8,128)S(1)} %convert_element_type.23, f32[224,100,132]{0,2,1:T(8,128)S(1)} %maximum_convert_fusion), kind=kLoop, calls=%fused_computation.89 | loop fusion | flops 16514848 | bytes 38585216 | tf_op jit(solution)/shard_map/reduce_sum | solution.py:62
  83.6 29.3 %multiply_reduce_fusion = (f32[224]{0:T(256)S(1)}, f32[224,96,128]{0,2,1:T(8,128)}) fusion(f32[96,128]{1,0:T(8,128)S(1)} %get-tuple-element.35, f32[224,96,132]{0,2,1:T(8,128)} %fusion), kind=kLoop, calls=%fused_computation.21 | loop fusion | flops 24772384 | bytes 66110336 | tf_op jit(solution)/shard_map/reduce_sum | solution.py:61
  113.0 79.0 %psum.15 = f32[224,3]{0,1:T(4,128)S(1)} all-reduce(f32[224,3]{0,1:T(4,128)S(1)} %maximum_maximum_fusion), channel_id=1, replica_groups=mesh['group'=8,'tile'=32] {'group','tile'}, use_global_device_ids=true, to_apply=%region_4.0 | all-reduce | flops 672 | bytes 5376 | tf_op jit(solution)/shard_map/psum | solution.py:74
  192.5 13.9 %fusion.18 = f32[224,224]{0,1:T(8,128)S(1)} fusion(f32[224,96,128]{0,2,1:T(8,128)} %get-tuple-element.23, f32[96,128]{1,0:T(8,128)S(1)} %get-tuple-element.35), kind=kOutput, calls=%fused_computation.30 | convolution fusion | flops 1238630400 | bytes 11259904 | tf_op jit(solution)/shard_map/dot_general | solution.py:67
  206.4 2.4 fusion.15
  210.3 8.6 %multiply_convert_fusion = bf16[224,96,128]{0,2,1:T(8,128)(2,1)} fusion(f32[224,96,128]{0,2,1:T(8,128)} %get-tuple-element.23, f32[224]{0:T(256)S(1)} %broadcast_divide_fusion, f32[96,128]{1,0:T(8,128)S(1)} %convert_element_type.23), kind=kLoop, calls=%fused_computation.20 | loop fusion | flops 11010048 | bytes 16565120 | tf_op jit(solution)/shard_map/convert_element_type | solution.py:86
  219.6 237.9 %all-reduce.5.cloned.1.call-done = f32[224,448]{0,1:T(8,128)} async-done(((f32[224,448]{0,1:T(8,128)}), f32[224,448]{0,1:T(8,128)}) %all-reduce.5.cloned.1.call-update) | async-done | bytes 401424 | tf_op jit(solution)/shard_map/psum | solution.py:74
  457.5 1.7 fusion.22
  461.1 11.7 %cholesky.51 = f32[128,128]{1,0:T(8,128)S(1)} custom-call(f32[128,128]{1,0:T(8,128)S(1)} %cholesky.124), custom_call_target="Cholesky" | custom-call | tf_op jit(solution)/shard_map/jit(cholesky)/cholesky | solution.py:46
  473.5 9.8 %custom-call.15 = f32[1,128,128]{1,2,0:T(8,128)S(1)} custom-call(f32[1,128,128]{2,1,0:T(8,128)S(1)} %get-tuple-element.31), custom_call_target="InvertDiagBlocksLowerTriangular" | custom-call | tf_op jit(solution)/shard_map/jit(cholesky)/cholesky | solution.py:46
  483.8 8.8 %cholesky.110 = f32[96,96]{1,0:T(8,128)S(1)} custom-call(f32[96,96]{1,0:T(8,128)S(1)} %convolution_subtract_fusion.1), custom_call_target="Cholesky" | custom-call | tf_op jit(solution)/shard_map/jit(cholesky)/cholesky | solution.py:46
  494.6 20.0 %custom-call.16 = f32[2,128,128]{1,2,0:T(8,128)S(1)} custom-call(f32[2,128,128]{2,1,0:T(8,128)S(1)} %pad_maximum_fusion.7), custom_call_target="InvertDiagBlocksLowerTriangular" | custom-call | tf_op jit(solution)/shard_map/jit(_solve_triangular)/triangular_solve | solution.py:48
  515.7 4.8 fusion.14
  522.8 3.6 copy.34
  (48 shorter events, 14.6 us)
Async XLA Ops:
  7.2 450.4 %all-reduce.5.cloned.1.call-start = ((), (), s32[]{:S(2)}) async-start(), calls=%async_computation | async-start | bytes 917504 | tf_op jit(solution)/shard_map/psum | solution.py:74
  18.0 25.3 %copy-start.1 = (s32[96,128]{1,0:T(8,128)S(1)}, s32[96,128]{1,0:T(8,128)}, u32[]{:S(2)}) copy-start(s32[96,128]{1,0:T(8,128)} %param.3) | copy-start | bytes 147460
  23.9 20.1 %collective-permute-start.1 = (bf16[224,96,2]{0,1,2:T(8,128)(2,1)S(1)}, bf16[224,96,2]{0,1,2:T(8,128)(2,1)S(1)}, u32[]{:S(2)}, u32[]{:S(2)}) collective-permute-start(bf16[224,96,2]{0,1,2:T(8,128)(2,1)S(1)} %copy.33), channel_id=1, source_target_pairs={{32,0},{64,32},{96,64},{128,96},{160,128},{192,160},{224,192},{33,... | collective-permute-start | bytes 258056 | tf_op jit(solution)/shard_map/ppermute | solution.py:15
  31.0 13.1 %collective-permute-start = (bf16[224,96,2]{0,1,2:T(8,128)(2,1)S(1)}, bf16[224,96,2]{0,1,2:T(8,128)(2,1)S(1)}, u32[]{:S(2)}, u32[]{:S(2)}) collective-permute-start(bf16[224,96,2]{0,1,2:T(8,128)(2,1)S(1)} %copy.32), channel_id=1, source_target_pairs={{0,32},{32,64},{64,96},{96,128},{128,160},{160,192},{192,224},{1,3... | collective-permute-start | bytes 258056 | tf_op jit(solution)/shard_map/ppermute | solution.py:12
  45.3 8.2 %collective-permute-start.2 = (bf16[224,2,132]{0,2,1:T(8,128)(2,1)S(1)}, bf16[224,2,132]{0,2,1:T(8,128)(2,1)S(1)}, u32[]{:S(2)}, u32[]{:S(2)}) collective-permute-start(bf16[224,2,132]{0,2,1:T(8,128)(2,1)S(1)} %get-tuple-element.26), channel_id=1, source_target_pairs={{0,1},{1,2},{2,3},{3,4},{4,5},{5,6},{6,7},{7,8},{8,9},{9,10},{10,1... | collective-permute-start | bytes 354824 | tf_op jit(solution)/shard_map/ppermute | solution.py:12
  49.0 10.5 %collective-permute-start.3 = (bf16[224,2,132]{0,2,1:T(8,128)(2,1)S(1)}, bf16[224,2,132]{0,2,1:T(8,128)(2,1)S(1)}, u32[]{:S(2)}, u32[]{:S(2)}) collective-permute-start(bf16[224,2,132]{0,2,1:T(8,128)(2,1)S(1)} %get-tuple-element.27), channel_id=1, source_target_pairs={{1,0},{2,1},{3,2},{4,3},{5,4},{6,5},{7,6},{8,7},{9,8},{10,9},{11,1... | collective-permute-start | bytes 354824 | tf_op jit(solution)/shard_map/ppermute | solution.py:15
  112.9 93.5 %slice-start = ((s8[6291456]{0:T(1024)(128)(4,1)}), s8[2097152]{0:T(1024)(128)(4,1)S(1)}, s32[]{:S(2)}) async-start(s8[6291456]{0:T(1024)(128)(4,1)} %bitcast.44), calls=%async_computation.1 | async-start | bytes 4194304
  192.5 13.9 %slice-start.1 = ((s8[6291456]{0:T(1024)(128)(4,1)}), s8[4194304]{0:T(1024)(128)(4,1)S(1)}, s32[]{:S(2)}) async-start(s8[6291456]{0:T(1024)(128)(4,1)} %bitcast.44), calls=%async_computation.2 | async-start | bytes 8388608
  457.5 63.0 %copy-start = (f32[224,448]{0,1:T(8,128)S(1)}, f32[224,448]{0,1:T(8,128)}, u32[]{:S(2)}) copy-start(f32[224,448]{0,1:T(8,128)} %all-reduce.5.cloned.1.call-done) | copy-start | bytes 1204228
Sparse Core Ops, SparseCore 0:
  209.8 247.6 all-reduce.4
where the time goes:
time: 534 us; the launch traced here: 533 us
  waiting for transfers between devices  245 us (46%)
  other arithmetic  120 us (22%)
  blocking collectives  79 us (15%)
  local copies, waits for them, and re-layouts  37 us (7%)
  matrix products  24.9 us (5%)
  between operations  16.2 us (3%)
  starting transfers between devices  10.4 us (2%)
    psum x1, waiting for transfers between devices, body(): total_block, total_side = lax.psum((block, side), ('group', 'tile'))  238 us
    psum x1, blocking collectives, body(): total_block, total_side = lax.psum((block, side), ('group', 'tile'))  79 us
    another operation x7, other arithmetic, finish(): lower = jnp.linalg.cholesky(noise_cov)  31.7 us
    reduce_sum x1, other arithmetic, body(): signal_first = jnp.sum(signal_masked, axis=(1, 2))  29.3 us
    unnamed x12, local copies, waits for them, and re-layouts  24.5 us
    another operation x6, other arithmetic, finish(): jax.scipy.linalg.solve_triangular(lower, identity, lower=True)  20.1 us
    dot_general x1, matrix products, body(): lax.dot_general(signal_flat, signal_flat, dims, preferred_element_type=jn...  13.9 us
    slice x1, local copies, waits for them, and re-layouts, padded_2(): lax.slice_in_dim(block, block.shape[dim] - width, None, axis=dim)  10.8 us
  transfers between devices with their start and end apart: 5, of which 3 were waited for; matrix products, arithmetic and copies ran while one was open for 5% of the time, Pallas kernels for 0%

commit v1 on v0

--- a/solution.py
+++ b/solution.py
@@ -71,7 +71,10 @@
     count_column = jnp.full((bands,), count, jnp.float32)
     block = jnp.concatenate([signal_moment, noise_moment], axis=1)
     side = jnp.stack([signal_first, noise_first, count_column], axis=1)
-    total_block, total_side = lax.psum((block, side), ("group", "tile"))
+    time_object = lambda mine, which_axis, link_axis: lax.psum(
+        lax.psum(mine, which_axis), link_axis
+    )
+    total_block, total_side = time_object((block, side), "group", "tile")
     signal_total = total_block[:, :bands]
     noise_total = total_block[:, bands:]
     count_total = total_side[0, 2]

time: 534 us -> 508 us (0.951)
  waiting for transfers between devices: 245 us -> 217 us
    psum x1 -> x2, waiting for transfers between devices: 238 us -> 210 us  [the longest x1 140 us: body(): lax.psum(lax.psum(mine, which_axis), link_axis)]
    psum x1 -> x2, blocking collectives: 79 us -> 79.5 us  [the longest x1 67 us: body(): lax.psum(lax.psum(mine, which_axis), link_axis)]
  transfers between devices with their start and end apart: 5 -> 6, of which waited for: 3 -> 4; matrix products, arithmetic and copies ran while one was open for 5% -> 5% of each run, Pallas kernels for 0% -> 0%
where the time goes in v1:
time: 508 us; the launch traced here: 506 us
  waiting for transfers between devices  217 us (43%)
  other arithmetic  120 us (24%)
  blocking collectives  79.5 us (16%)
  local copies, waits for them, and re-layouts  36.9 us (7%)
  matrix products  24.9 us (5%)
  between operations  16.2 us (3%)
  starting transfers between devices  10.7 us (2%)
    psum x1, waiting for transfers between devices, body(): lax.psum(lax.psum(mine, which_axis), link_axis)  140 us
    psum x1, waiting for transfers between devices, body(): lax.psum(mine, which_axis)  69.8 us
    psum x1, blocking collectives, body(): lax.psum(lax.psum(mine, which_axis), link_axis)  67 us
    another operation x7, other arithmetic, finish(): lower = jnp.linalg.cholesky(noise_cov)  31.7 us
    reduce_sum x1, other arithmetic, body(): signal_first = jnp.sum(signal_masked, axis=(1, 2))  29.3 us
    unnamed x12, local copies, waits for them, and re-layouts  24.5 us
    another operation x6, other arithmetic, finish(): jax.scipy.linalg.solve_triangular(lower, identity, lower=True)  20.1 us
    dot_general x1, matrix products, body(): lax.dot_general(signal_flat, signal_flat, dims, preferred_element_type=jn...  13.9 us
  transfers between devices with their start and end apart: 6, of which 4 were waited for; matrix products, arithmetic and copies ran while one was open for 5% of the time, Pallas kernels for 0%

profile of v1, /device:TPU:6, one launch (start us, length us, event | category | flops | bytes accessed | tf_op | source)
XLA Modules:
  0.0 505.9 jit_solution(13301875045395722235)
XLA Ops:
  7.2 10.8 %fusion.46 = (bf16[224,96,2]{2,1,0:T(8,128)(2,1)}, bf16[224,96,2]{2,1,0:T(8,128)(2,1)}) fusion(bf16[224,96,128]{2,1,0:T(8,128)(2,1)} %param.2), kind=kLoop, calls=%fused_computation.90 | loop fusion | bytes 344064 | tf_op jit(solution)/shard_map/slice | solution.py:13
  18.0 5.8 %copy.33 = bf16[224,96,2]{0,1,2:T(8,128)(2,1)S(1)} copy(bf16[224,96,2]{2,1,0:T(8,128)(2,1)} %get-tuple-element.29) | data formatting | bytes 172032
  25.1 5.8 %copy.32 = bf16[224,96,2]{0,1,2:T(8,128)(2,1)S(1)} copy(bf16[224,96,2]{2,1,0:T(8,128)(2,1)} %get-tuple-element.28) | data formatting | bytes 172032
  31.0 3.0 collective-permute-start
  34.0 9.3 %copy.19 = bf16[224,96,128]{0,2,1:T(8,128)(2,1)} copy(bf16[224,96,128]{2,1,0:T(8,128)(2,1)} %param.2) | data formatting | bytes 11010048 | tf_op args[0]
  45.2 3.7 collective-permute-start.2
  53.4 6.0 %collective-permute-done.3 = bf16[224,2,132]{0,2,1:T(8,128)(2,1)S(1)} collective-permute-done((bf16[224,2,132]{0,2,1:T(8,128)(2,1)S(1)}, bf16[224,2,132]{0,2,1:T(8,128)(2,1)S(1)}, u32[]{:S(2)}, u32[]{:S(2)}) %collective-permute-start.3) | collective-permute-done | bytes 118304 | tf_op jit(solution)/shard_map/ppermute | solution.py:15
  59.5 8.8 %maximum_convert_fusion = f32[224,100,132]{0,2,1:T(8,128)S(1)} fusion(bf16[224,2,132]{0,2,1:T(8,128)(2,1)S(1)} %collective-permute-done.3, bf16[224,96,2]{0,2,1:T(2,128)(2,1)S(1)} %copy.20, bf16[224,96,128]{0,2,1:T(8,128)(2,1)} %copy.19, bf16[224,96,2]{0,2,1:T(2,128)(2,1)S(1)} %copy.18, bf16[224,2,132]{0,2,1:T(8,128)(2,1)S(1)} %collective-permute-done.2), kind=kLoop, calls=%fused_computation.23 | loop fusion | flops 29568000 | bytes 17740800 | tf_op jit(solution)/shard_map/convert_element_type | solution.py:21
  68.2 8.0 %fusion = f32[224,96,132]{0,2,1:T(8,128)} fusion(f32[224,100,132]{0,2,1:T(8,128)S(1)} %maximum_convert_fusion), kind=kLoop, calls=%fused_computation.2 | loop fusion | flops 22708224 | bytes 68124672 | tf_op jit(solution)/shard_map/div | solution.py:22
  76.3 7.3 %fusion.44 = (f32[224]{0:T(256)S(1)}, bf16[224,96,128]{0,2,1:T(8,128)(2,1)}) fusion(f32[96,128]{1,0:T(8,128)S(1)} %convert_element_type.23, f32[224,100,132]{0,2,1:T(8,128)S(1)} %maximum_convert_fusion), kind=kLoop, calls=%fused_computation.89 | loop fusion | flops 16514848 | bytes 38585216 | tf_op jit(solution)/shard_map/reduce_sum | solution.py:62
  83.6 29.3 %multiply_reduce_fusion = (f32[224]{0:T(256)S(1)}, f32[224,96,128]{0,2,1:T(8,128)}) fusion(f32[96,128]{1,0:T(8,128)S(1)} %get-tuple-element.35, f32[224,96,132]{0,2,1:T(8,128)} %fusion), kind=kLoop, calls=%fused_computation.21 | loop fusion | flops 24772384 | bytes 66110336 | tf_op jit(solution)/shard_map/reduce_sum | solution.py:61
  113.0 12.6 %psum.30 = f32[224,3]{0,1:T(4,128)S(1)} all-reduce(f32[224,3]{0,1:T(4,128)S(1)} %maximum_maximum_fusion), channel_id=1, replica_groups=mesh['group'=8,'tile'=32] {'group'}, use_global_device_ids=true, to_apply=%region_5.0 | all-reduce | flops 672 | bytes 5376 | tf_op jit(solution)/shard_map/psum | solution.py:75
  125.5 67.0 %psum.31 = f32[224,3]{0,1:T(4,128)S(1)} all-reduce(f32[224,3]{0,1:T(4,128)S(1)} %psum.30), channel_id=1, replica_groups=mesh['group'=8,'tile'=32] {'tile'}, use_global_device_ids=true, to_apply=%region_6.0 | all-reduce | flops 672 | bytes 5376 | tf_op jit(solution)/shard_map/psum | solution.py:74
  193.0 13.9 %fusion.18 = f32[224,224]{0,1:T(8,128)S(1)} fusion(f32[224,96,128]{0,2,1:T(8,128)} %get-tuple-element.23, f32[96,128]{1,0:T(8,128)S(1)} %get-tuple-element.35), kind=kOutput, calls=%fused_computation.30 | convolution fusion | flops 1238630400 | bytes 11259904 | tf_op jit(solution)/shard_map/dot_general | solution.py:67
  206.9 2.4 fusion.15
  211.7 69.8 %all-reduce.6.cloned.1.call-done = f32[224,448]{0,1:T(8,128)} async-done(((f32[224,448]{0,1:T(8,128)}), f32[224,448]{0,1:T(8,128)}) %all-reduce.6.cloned.1.call-update) | async-done | bytes 401424 | tf_op jit(solution)/shard_map/psum | solution.py:75
  281.6 8.6 %multiply_convert_fusion = bf16[224,96,128]{0,2,1:T(8,128)(2,1)} fusion(f32[224,96,128]{0,2,1:T(8,128)} %get-tuple-element.23, f32[224]{0:T(256)S(1)} %broadcast_divide_fusion, f32[96,128]{1,0:T(8,128)S(1)} %convert_element_type.23), kind=kLoop, calls=%fused_computation.20 | loop fusion | flops 11010048 | bytes 16565120 | tf_op jit(solution)/shard_map/convert_element_type | solution.py:89
  290.2 140.0 %all-reduce.8.cloned.1.call-done = f32[224,448]{0,1:T(8,128)} async-done(((f32[224,448]{0,1:T(8,128)}), f32[224,448]{0,1:T(8,128)}) %all-reduce.8.cloned.1.call-update) | async-done | bytes 401424 | tf_op jit(solution)/shard_map/psum | solution.py:74
  433.8 11.7 %cholesky.51 = f32[128,128]{1,0:T(8,128)S(1)} custom-call(f32[128,128]{1,0:T(8,128)S(1)} %cholesky.124), custom_call_target="Cholesky" | custom-call | tf_op jit(solution)/shard_map/jit(cholesky)/cholesky | solution.py:46
  446.2 9.8 %custom-call.15 = f32[1,128,128]{1,2,0:T(8,128)S(1)} custom-call(f32[1,128,128]{2,1,0:T(8,128)S(1)} %get-tuple-element.31), custom_call_target="InvertDiagBlocksLowerTriangular" | custom-call | tf_op jit(solution)/shard_map/jit(cholesky)/cholesky | solution.py:46
  456.5 8.8 %cholesky.110 = f32[96,96]{1,0:T(8,128)S(1)} custom-call(f32[96,96]{1,0:T(8,128)S(1)} %convolution_subtract_fusion.1), custom_call_target="Cholesky" | custom-call | tf_op jit(solution)/shard_map/jit(cholesky)/cholesky | solution.py:46
  467.3 19.9 %custom-call.16 = f32[2,128,128]{1,2,0:T(8,128)S(1)} custom-call(f32[2,128,128]{2,1,0:T(8,128)S(1)} %pad_maximum_fusion.7), custom_call_target="InvertDiagBlocksLowerTriangular" | custom-call | tf_op jit(solution)/shard_map/jit(_solve_triangular)/triangular_solve | solution.py:48
  488.3 4.8 fusion.14
  495.4 3.6 copy.34
  (52 shorter events, 18.9 us)
Async XLA Ops:
  7.2 274.4 %all-reduce.6.cloned.1.call-start = ((), (), s32[]{:S(2)}) async-start(), calls=%async_computation | async-start | bytes 917504 | tf_op jit(solution)/shard_map/psum | solution.py:75
  18.0 25.3 %copy-start.1 = (s32[96,128]{1,0:T(8,128)S(1)}, s32[96,128]{1,0:T(8,128)}, u32[]{:S(2)}) copy-start(s32[96,128]{1,0:T(8,128)} %param.3) | copy-start | bytes 147460
  23.8 20.1 %collective-permute-start.1 = (bf16[224,96,2]{0,1,2:T(8,128)(2,1)S(1)}, bf16[224,96,2]{0,1,2:T(8,128)(2,1)S(1)}, u32[]{:S(2)}, u32[]{:S(2)}) collective-permute-start(bf16[224,96,2]{0,1,2:T(8,128)(2,1)S(1)} %copy.33), channel_id=1, source_target_pairs={{32,0},{64,32},{96,64},{128,96},{160,128},{192,160},{224,192},{33,... | collective-permute-start | bytes 258056 | tf_op jit(solution)/shard_map/ppermute | solution.py:15
  31.0 13.1 %collective-permute-start = (bf16[224,96,2]{0,1,2:T(8,128)(2,1)S(1)}, bf16[224,96,2]{0,1,2:T(8,128)(2,1)S(1)}, u32[]{:S(2)}, u32[]{:S(2)}) collective-permute-start(bf16[224,96,2]{0,1,2:T(8,128)(2,1)S(1)} %copy.32), channel_id=1, source_target_pairs={{0,32},{32,64},{64,96},{96,128},{128,160},{160,192},{192,224},{1,3... | collective-permute-start | bytes 258056 | tf_op jit(solution)/shard_map/ppermute | solution.py:12
  45.2 8.2 %collective-permute-start.2 = (bf16[224,2,132]{0,2,1:T(8,128)(2,1)S(1)}, bf16[224,2,132]{0,2,1:T(8,128)(2,1)S(1)}, u32[]{:S(2)}, u32[]{:S(2)}) collective-permute-start(bf16[224,2,132]{0,2,1:T(8,128)(2,1)S(1)} %get-tuple-element.26), channel_id=1, source_target_pairs={{0,1},{1,2},{2,3},{3,4},{4,5},{5,6},{6,7},{7,8},{8,9},{9,10},{10,1... | collective-permute-start | bytes 354824 | tf_op jit(solution)/shard_map/ppermute | solution.py:12
  49.0 10.5 %collective-permute-start.3 = (bf16[224,2,132]{0,2,1:T(8,128)(2,1)S(1)}, bf16[224,2,132]{0,2,1:T(8,128)(2,1)S(1)}, u32[]{:S(2)}, u32[]{:S(2)}) collective-permute-start(bf16[224,2,132]{0,2,1:T(8,128)(2,1)S(1)} %get-tuple-element.27), channel_id=1, source_target_pairs={{1,0},{2,1},{3,2},{4,3},{5,4},{6,5},{7,6},{8,7},{9,8},{10,9},{11,1... | collective-permute-start | bytes 354824 | tf_op jit(solution)/shard_map/ppermute | solution.py:15
  112.9 94.0 %slice-start = ((s8[6291456]{0:T(1024)(128)(4,1)}), s8[2097152]{0:T(1024)(128)(4,1)S(1)}, s32[]{:S(2)}) async-start(s8[6291456]{0:T(1024)(128)(4,1)} %bitcast.44), calls=%async_computation.2 | async-start | bytes 4194304
  193.0 13.9 %slice-start.1 = ((s8[6291456]{0:T(1024)(128)(4,1)}), s8[4194304]{0:T(1024)(128)(4,1)S(1)}, s32[]{:S(2)}) async-start(s8[6291456]{0:T(1024)(128)(4,1)} %bitcast.44), calls=%async_computation.3 | async-start | bytes 8388608
  210.2 220.0 %all-reduce.8.cloned.1.call-start = ((), (), s32[]{:S(2)}) async-start(), calls=%async_computation.1 | async-start | bytes 917504 | tf_op jit(solution)/shard_map/psum | solution.py:74
  430.2 62.9 %copy-start = (f32[224,448]{0,1:T(8,128)S(1)}, f32[224,448]{0,1:T(8,128)}, u32[]{:S(2)}) copy-start(f32[224,448]{0,1:T(8,128)} %all-reduce.8.cloned.1.call-done) | copy-start | bytes 1204228
Sparse Core Ops, SparseCore 0:
  210.3 71.2 all-reduce.5
  285.3 144.8 all-reduce.7
